TPU v7x, 256 devices: a whole 4x4x8 slice. The times are simulated.
256 devices in a mesh: row: 16 (over x, y), col: 16 (over z, core).
Axes of the slice: x: 4, y: 4, z: 8, core: 2. Of those that a mesh axis runs over, the one named last changes fastest.
Arguments:
- features: bfloat16 [65536, 256], P(('col', 'row')), may hold values from -6 to 6
- cotangent: bfloat16 [65536, 256], P(('row', 'col')), may hold values from -1.5 to 1.5
- degrees: int32 [65536], P(('row', 'col')), may hold values from 8 to 40
- weight: bfloat16 [256, 256], replicated, may hold values from -0.375 to 0.375
- tile_rows: int32 [16, 16, 256], P('row', 'col'), may hold values from 0 to 31
- tile_cols: int32 [16, 16, 256], P('row', 'col'), may hold values from 0 to 31
- tile_bits: int32 [16, 16, 256, 16, 128], P('row', 'col'), may hold values from 0 to 255, as said below
- tile_count: int32 [16, 16], P('row', 'col'), may hold values from 16 to 256, as said below
Outputs:
- output: bfloat16 [65536, 256], P(('row', 'col'))
- weight_grad: float32 [256, 256], replicated
- input_grad: bfloat16 [65536, 256], P(('col', 'row'))
Inputs may be any that keep to these rules, and one draw needn't show every extreme that they name: `tile_bits`: each word holds 8 entries of 0 or 1 in its low bits; tiles at the same position may repeat and then add. `tile_count`: some device has all 256 slots live and some device 256 // 16.
All inputs are finite; a program needn't handle non-finite values.
Results may differ from a plain program's by a relative error of at most 0.024.
Values may be sent and summed in bfloat16 or wider, within the bound.
No kernel may reach another device: no remote copies, remote signals or barrier semaphores. Data moves between devices by JAX's collectives and lax.ppermute only.
A program may use at most 64 MiB of HBM per device.

v0:
```python
import math
import jax
import jax.numpy as jnp
from jax import lax
from jax.sharding import PartitionSpec as P


def unpack(packed):
    shifts = jnp.arange(8, dtype=jnp.int32)
    flags = jnp.right_shift(packed[:, :, None, :], shifts[None, None, :, None]) & 1
    return flags.reshape(packed.shape[0], packed.shape[1] * 8, packed.shape[2])


def sweep_tiles(packed, row_ids, col_ids, live_count, source, tile_offset, out_tiles, forward):
    tile_size = packed.shape[-1]
    feature_width = source.shape[-1]
    block_size = math.gcd(packed.shape[0], 32)

    def one_block(position, totals):
        offset = position * block_size
        block_bits = lax.dynamic_slice_in_dim(packed, offset, block_size, 0)
        block_rows = lax.dynamic_slice_in_dim(row_ids, offset, block_size, 0)
        block_cols = lax.dynamic_slice_in_dim(col_ids, offset, block_size, 0)
        if forward:
            target = block_rows - tile_offset
        else:
            target = block_cols - tile_offset
        inside = (target >= 0) & (target < out_tiles)
        live_mask = (offset + jnp.arange(block_size, dtype=jnp.int32) < live_count) & inside
        placed = jnp.clip(target, 0, out_tiles - 1)
        pattern = (unpack(block_bits) * live_mask.astype(jnp.int32)[:, None, None]).astype(
            jnp.bfloat16
        )
        if forward:
            product = jnp.einsum(
                "bji,bjf->bif", pattern, source[block_cols], preferred_element_type=jnp.float32
            )
        else:
            product = jnp.einsum(
                "bji,bif->bjf", pattern, source[block_rows], preferred_element_type=jnp.float32
            )
        return totals.at[placed].add(product)

    initial = jnp.zeros((out_tiles, tile_size, feature_width), jnp.float32)
    blocks_used = packed.shape[0] // block_size
    return lax.fori_loop(0, blocks_used, one_block, initial)


def forward_pass(features, degrees, weight, packed, row_ids, col_ids, live_count):
    tile_size = packed.shape[-1]
    width = features.shape[-1]
    gathered = lax.all_gather(features, "row", axis=0, tiled=True)
    source = gathered.reshape(-1, tile_size, width)
    out_tiles = features.shape[0] * lax.axis_size("col") // tile_size
    partial_value = sweep_tiles(packed, row_ids, col_ids, live_count, source, 0, out_tiles, True)
    summed = lax.psum_scatter(
        partial_value.reshape(-1, width).astype(jnp.bfloat16),
        "col",
        scatter_dimension=0,
        tiled=True,
    ).astype(jnp.float32)
    aggregated = (summed / degrees[:, None].astype(jnp.float32)).astype(jnp.bfloat16)
    output = jnp.dot(aggregated, weight, preferred_element_type=jnp.float32).astype(jnp.bfloat16)
    return (aggregated, output)


def backward_pass(cotangent, degrees, weight, packed, row_ids, col_ids, live_count):
    tile_size = packed.shape[-1]
    width = cotangent.shape[-1]
    scaled = (cotangent.astype(jnp.float32) / degrees[:, None].astype(jnp.float32)).astype(
        jnp.bfloat16
    )
    gathered = lax.all_gather(scaled, "col", axis=0, tiled=True)
    source = gathered.reshape(-1, tile_size, width)
    out_tiles = cotangent.shape[0] * lax.axis_size("row") // tile_size
    partial_value = sweep_tiles(packed, row_ids, col_ids, live_count, source, 0, out_tiles, False)
    summed = lax.psum_scatter(
        partial_value.reshape(-1, width).astype(jnp.bfloat16),
        "row",
        scatter_dimension=0,
        tiled=True,
    )
    return jnp.dot(summed, weight.T, preferred_element_type=jnp.float32).astype(jnp.bfloat16)


def per_device(features, cotangent, degrees, weight, tile_rows, tile_cols, tile_bits, tile_count):
    packed = tile_bits[0, 0]
    row_ids = tile_rows[0, 0]
    col_ids = tile_cols[0, 0]
    live_count = tile_count[0, 0]
    aggregated, output = forward_pass(
        features, degrees, weight, packed, row_ids, col_ids, live_count
    )
    input_grad = backward_pass(cotangent, degrees, weight, packed, row_ids, col_ids, live_count)
    local_term = lax.dot_general(
        aggregated, cotangent, (((0,), (0,)), ((), ())), preferred_element_type=jnp.float32
    )
    weight_grad = lax.psum(local_term, ("row", "col"))
    return (output, weight_grad, input_grad)


def solution(mesh):
    placed = (
        P(("col", "row"), None),
        P(("row", "col"), None),
        P(("row", "col")),
        P(),
        P("row", "col", None),
        P("row", "col", None),
        P("row", "col", None, None, None),
        P("row", "col"),
    )
    return jax.shard_map(
        per_device,
        mesh=mesh,
        in_specs=placed,
        out_specs=(P(("row", "col"), None), P(), P(("col", "row"), None)),
        check_vma=False,
    )
```

profile of v0, /device:TPU:2, one launch (start us, length us, event | category | flops | bytes accessed | tf_op | source)
XLA Modules:
  0.0 690.2 jit_solution(7609712674612229882)
XLA Ops:
  8.6 1.7 divide_convert_fusion
  10.4 52.7 %all-gather.3.cloned.1.call-done = bf16[4096,256]{1,0:T(8,128)(2,1)} async-done(((bf16[256,256]{1,0:T(8,128)(2,1)}), bf16[4096,256]{1,0:T(8,128)(2,1)}) %all-gather.3.cloned.1.call-update) | async-done | bytes 2097168 | tf_op jit(solution)/shard_map/all_gather | solution.py:52
  63.1 2.5 broadcast.54.clone
  65.5 136.1 %while.26 = (s32[]{:T(128)}, f32[32,128,256]{2,1,0:T(8,128)}, s32[256]{0:T(256)S(1)}, s32[256,16,128]{2,1,0:T(8,128)}, s32[]{:T(128)}, /*index=5*/s32[256]{0:T(2...) while((s32[]{:T(128)}, f32[32,128,256]{2,1,0:T(8,128)}, ...), condition=%wide.region_2.3_spmd, body=%wide.region_0.2_spmd.sunk | while | flops 271582656 | bytes 23862704 | solution.py:46
  66.3 2.3 gather_fusion
  69.7 2.9 fusion.35
  72.6 10.0 %scatter_fusion = f32[32,128,256]{2,1,0:T(8,128)} fusion(f32[32,128,256]{2,1,0:T(8,128)} %get-tuple-element.398, s32[32]{0:T(128)S(1)} %get-tuple-element.375, f32[32,128,256]{2,1,0:T(8,128)} %fusion.35), kind=kCustom, calls=%fused_computation.2.clone.1 | custom fusion | flops 1048576 | bytes 12583040 | tf_op jit(solution)/shard_map/while/body/eval_jaxpr/scatter-add | solution.py:42
  83.5 2.3 gather_fusion
  86.8 2.9 fusion.35
  89.7 10.0 %scatter_fusion = f32[32,128,256]{2,1,0:T(8,128)} fusion(f32[32,128,256]{2,1,0:T(8,128)} %get-tuple-element.398, s32[32]{0:T(128)S(1)} %get-tuple-element.375, f32[32,128,256]{2,1,0:T(8,128)} %fusion.35), kind=kCustom, calls=%fused_computation.2.clone.1 | custom fusion | flops 1048576 | bytes 12583040 | tf_op jit(solution)/shard_map/while/body/eval_jaxpr/scatter-add | solution.py:42
  100.5 2.3 gather_fusion
  102.8 1.0 constant_dynamic-slice_fusion.4
  103.9 2.9 fusion.35
  106.8 9.8 %scatter_fusion = f32[32,128,256]{2,1,0:T(8,128)} fusion(f32[32,128,256]{2,1,0:T(8,128)} %get-tuple-element.398, s32[32]{0:T(128)S(1)} %get-tuple-element.375, f32[32,128,256]{2,1,0:T(8,128)} %fusion.35), kind=kCustom, calls=%fused_computation.2.clone.1 | custom fusion | flops 1048576 | bytes 12583040 | tf_op jit(solution)/shard_map/while/body/eval_jaxpr/scatter-add | solution.py:42
  117.4 2.3 gather_fusion
  120.7 2.9 fusion.35
  123.6 9.9 %scatter_fusion = f32[32,128,256]{2,1,0:T(8,128)} fusion(f32[32,128,256]{2,1,0:T(8,128)} %get-tuple-element.398, s32[32]{0:T(128)S(1)} %get-tuple-element.375, f32[32,128,256]{2,1,0:T(8,128)} %fusion.35), kind=kCustom, calls=%fused_computation.2.clone.1 | custom fusion | flops 1048576 | bytes 12583040 | tf_op jit(solution)/shard_map/while/body/eval_jaxpr/scatter-add | solution.py:42
  134.3 2.3 gather_fusion
  137.7 2.9 fusion.35
  140.6 9.9 %scatter_fusion = f32[32,128,256]{2,1,0:T(8,128)} fusion(f32[32,128,256]{2,1,0:T(8,128)} %get-tuple-element.398, s32[32]{0:T(128)S(1)} %get-tuple-element.375, f32[32,128,256]{2,1,0:T(8,128)} %fusion.35), kind=kCustom, calls=%fused_computation.2.clone.1 | custom fusion | flops 1048576 | bytes 12583040 | tf_op jit(solution)/shard_map/while/body/eval_jaxpr/scatter-add | solution.py:42
  151.3 2.3 gather_fusion
  154.6 2.9 fusion.35
  157.5 10.0 %scatter_fusion = f32[32,128,256]{2,1,0:T(8,128)} fusion(f32[32,128,256]{2,1,0:T(8,128)} %get-tuple-element.398, s32[32]{0:T(128)S(1)} %get-tuple-element.375, f32[32,128,256]{2,1,0:T(8,128)} %fusion.35), kind=kCustom, calls=%fused_computation.2.clone.1 | custom fusion | flops 1048576 | bytes 12583040 | tf_op jit(solution)/shard_map/while/body/eval_jaxpr/scatter-add | solution.py:42
  168.4 2.3 gather_fusion
  171.7 2.9 fusion.35
  174.6 10.0 %scatter_fusion = f32[32,128,256]{2,1,0:T(8,128)} fusion(f32[32,128,256]{2,1,0:T(8,128)} %get-tuple-element.398, s32[32]{0:T(128)S(1)} %get-tuple-element.375, f32[32,128,256]{2,1,0:T(8,128)} %fusion.35), kind=kCustom, calls=%fused_computation.2.clone.1 | custom fusion | flops 1048576 | bytes 12583040 | tf_op jit(solution)/shard_map/while/body/eval_jaxpr/scatter-add | solution.py:42
  185.5 2.3 gather_fusion
  188.8 2.9 fusion.35
  191.7 9.9 %scatter_fusion = f32[32,128,256]{2,1,0:T(8,128)} fusion(f32[32,128,256]{2,1,0:T(8,128)} %get-tuple-element.398, s32[32]{0:T(128)S(1)} %get-tuple-element.375, f32[32,128,256]{2,1,0:T(8,128)} %fusion.35), kind=kCustom, calls=%fused_computation.2.clone.1 | custom fusion | flops 1048576 | bytes 12583040 | tf_op jit(solution)/shard_map/while/body/eval_jaxpr/scatter-add | solution.py:42
  201.6 3.8 convert_element_type.63
  205.5 2.5 broadcast.54.clone.1
  208.0 134.8 %while.27 = (s32[]{:T(128)}, f32[32,128,256]{2,1,0:T(8,128)}, s32[256]{0:T(256)S(1)}, s32[256,16,128]{2,1,0:T(8,128)}, s32[]{:T(128)}, /*index=5*/s32[256]{0:T(2...) while((s32[]{:T(128)}, f32[32,128,256]{2,1,0:T(8,128)}, ...), condition=%wide.region_7.8_spmd, body=%wide.region_5.7_spmd.sunk | while | flops 271582656 | bytes 23862704 | solution.py:46
  208.8 2.3 gather_fusion.1
  212.2 2.7 fusion.38
  214.9 10.2 %scatter_fusion.1 = f32[32,128,256]{2,1,0:T(8,128)} fusion(f32[32,128,256]{2,1,0:T(8,128)} %get-tuple-element.431, s32[32]{0:T(128)S(1)} %get-tuple-element.384, f32[32,128,256]{2,1,0:T(8,128)} %fusion.38), kind=kCustom, calls=%fused_computation.3.clone.1 | custom fusion | flops 1048576 | bytes 12583040 | tf_op jit(solution)/shard_map/while/body/eval_jaxpr/scatter-add | solution.py:42
  225.9 2.3 gather_fusion.1
  229.3 2.7 fusion.38
  232.0 9.8 %scatter_fusion.1 = f32[32,128,256]{2,1,0:T(8,128)} fusion(f32[32,128,256]{2,1,0:T(8,128)} %get-tuple-element.431, s32[32]{0:T(128)S(1)} %get-tuple-element.384, f32[32,128,256]{2,1,0:T(8,128)} %fusion.38), kind=kCustom, calls=%fused_computation.3.clone.1 | custom fusion | flops 1048576 | bytes 12583040 | tf_op jit(solution)/shard_map/while/body/eval_jaxpr/scatter-add | solution.py:42
  242.6 2.3 gather_fusion.1
  244.9 1.0 constant_dynamic-slice_fusion.5
  246.0 2.7 fusion.38
  248.7 10.0 %scatter_fusion.1 = f32[32,128,256]{2,1,0:T(8,128)} fusion(f32[32,128,256]{2,1,0:T(8,128)} %get-tuple-element.431, s32[32]{0:T(128)S(1)} %get-tuple-element.384, f32[32,128,256]{2,1,0:T(8,128)} %fusion.38), kind=kCustom, calls=%fused_computation.3.clone.1 | custom fusion | flops 1048576 | bytes 12583040 | tf_op jit(solution)/shard_map/while/body/eval_jaxpr/scatter-add | solution.py:42
  259.5 2.3 gather_fusion.1
  262.8 2.7 fusion.38
  265.5 9.9 %scatter_fusion.1 = f32[32,128,256]{2,1,0:T(8,128)} fusion(f32[32,128,256]{2,1,0:T(8,128)} %get-tuple-element.431, s32[32]{0:T(128)S(1)} %get-tuple-element.384, f32[32,128,256]{2,1,0:T(8,128)} %fusion.38), kind=kCustom, calls=%fused_computation.3.clone.1 | custom fusion | flops 1048576 | bytes 12583040 | tf_op jit(solution)/shard_map/while/body/eval_jaxpr/scatter-add | solution.py:42
  276.2 2.3 gather_fusion.1
  279.6 2.7 fusion.38
  282.3 9.9 %scatter_fusion.1 = f32[32,128,256]{2,1,0:T(8,128)} fusion(f32[32,128,256]{2,1,0:T(8,128)} %get-tuple-element.431, s32[32]{0:T(128)S(1)} %get-tuple-element.384, f32[32,128,256]{2,1,0:T(8,128)} %fusion.38), kind=kCustom, calls=%fused_computation.3.clone.1 | custom fusion | flops 1048576 | bytes 12583040 | tf_op jit(solution)/shard_map/while/body/eval_jaxpr/scatter-add | solution.py:42
  293.0 2.3 gather_fusion.1
  296.3 2.7 fusion.38
  299.0 10.0 %scatter_fusion.1 = f32[32,128,256]{2,1,0:T(8,128)} fusion(f32[32,128,256]{2,1,0:T(8,128)} %get-tuple-element.431, s32[32]{0:T(128)S(1)} %get-tuple-element.384, f32[32,128,256]{2,1,0:T(8,128)} %fusion.38), kind=kCustom, calls=%fused_computation.3.clone.1 | custom fusion | flops 1048576 | bytes 12583040 | tf_op jit(solution)/shard_map/while/body/eval_jaxpr/scatter-add | solution.py:42
  309.8 2.3 gather_fusion.1
  313.2 2.7 fusion.38
  315.9 10.1 %scatter_fusion.1 = f32[32,128,256]{2,1,0:T(8,128)} fusion(f32[32,128,256]{2,1,0:T(8,128)} %get-tuple-element.431, s32[32]{0:T(128)S(1)} %get-tuple-element.384, f32[32,128,256]{2,1,0:T(8,128)} %fusion.38), kind=kCustom, calls=%fused_computation.3.clone.1 | custom fusion | flops 1048576 | bytes 12583040 | tf_op jit(solution)/shard_map/while/body/eval_jaxpr/scatter-add | solution.py:42
  326.8 2.3 gather_fusion.1
  330.1 2.7 fusion.38
  332.8 10.0 %scatter_fusion.1 = f32[32,128,256]{2,1,0:T(8,128)} fusion(f32[32,128,256]{2,1,0:T(8,128)} %get-tuple-element.431, s32[32]{0:T(128)S(1)} %get-tuple-element.384, f32[32,128,256]{2,1,0:T(8,128)} %fusion.38), kind=kCustom, calls=%fused_computation.3.clone.1 | custom fusion | flops 1048576 | bytes 12583040 | tf_op jit(solution)/shard_map/while/body/eval_jaxpr/scatter-add | solution.py:42
  342.9 3.8 convert_element_type.71
  347.6 1.9 fusion.20
  349.6 1.8 convolution_convert_fusion.1
  351.4 73.8 %reduce-scatter.5.cloned.1.call-done = bf16[256,256]{1,0:T(8,128)(2,1)} async-done(((bf16[4096,256]{1,0:T(8,128)(2,1)}), bf16[256,256]{1,0:T(8,128)(2,1)}) %reduce-scatter.5.cloned.1.call-update) | async-done | bytes 131088 | tf_op jit(solution)/shard_map/reduce_scatter | solution.py:77
  425.1 1.8 convolution_convert_fusion
  426.9 255.1 %all-reduce.2.cloned.1.call-done = f32[256,256]{1,0:T(8,128)} async-done(((f32[256,256]{1,0:T(8,128)}), f32[256,256]{1,0:T(8,128)}) %all-reduce.2.cloned.1.call-update) | async-done | bytes 262160 | tf_op jit(solution)/shard_map/psum | solution.py:98
  682.0 1.7 copy.29
  (115 shorter events, 30.4 us)
Async XLA Ops:
  7.2 342.4 %copy-start = (bf16[256,256]{1,0:T(8,128)(2,1)S(1)}, bf16[256,256]{1,0:T(8,128)(2,1)}, u32[]{:S(2)}) copy-start(bf16[256,256]{1,0:T(8,128)(2,1)} %param.15) | copy-start | bytes 393220
  7.2 55.9 %all-gather.3.cloned.1.call-start = ((), (), s32[]{:S(2)}) async-start(), calls=%async_computation.2 | async-start | bytes 2228224 | tf_op jit(solution)/shard_map/all_gather | solution.py:52
  7.9 197.6 %all-gather.5.cloned.1.call-start = ((), (), s32[]{:S(2)}) async-start(), calls=%async_computation.5 | async-start | bytes 2228224 | tf_op jit(solution)/shard_map/all_gather | solution.py:73
  10.3 336.5 %reduce-scatter.3.cloned.1.call-start = ((), (), s32[]{:S(2)}) async-start(), calls=%async_computation.3 | async-start | bytes 2228224 | tf_op jit(solution)/shard_map/reduce_scatter | solution.py:56
  63.1 2.5 copy-start.2
  63.1 2.5 copy-start.3
  205.5 219.7 %reduce-scatter.5.cloned.1.call-start = ((), (), s32[]{:S(2)}) async-start(), calls=%async_computation.6 | async-start | bytes 2228224 | tf_op jit(solution)/shard_map/reduce_scatter | solution.py:77
  346.7 0.9 copy-start.1
  346.7 335.2 %all-reduce.2.cloned.1.call-start = ((), (), s32[]{:S(2)}) async-start(), calls=%async_computation.4 | async-start | bytes 524288 | tf_op jit(solution)/shard_map/psum | solution.py:98
Sparse Core Ops, SparseCore 0:
  10.4 52.5 all-gather.2
  65.5 39.5 all-gather.4
  205.6 59.0 reduce-scatter.2
  346.9 78.2 reduce-scatter.4
  431.9 250.0 all-reduce.1
where the time goes:
time: 692 us; the launch traced here: 690 us
  waiting for transfers between devices  382 us (55%)
  other arithmetic  182 us (26%)
  local copies, waits for them, and re-layouts  60.8 us (9%)
  matrix products  50.3 us (7%)
  between operations  13.8 us (2%)
    psum x1, waiting for transfers between devices, per_device(): weight_grad = lax.psum(local_term, ('row', 'col'))  255 us
    scatter-add x16, other arithmetic, one_block(): return totals.at[placed].add(product)  159 us
    reduce_scatter x1, waiting for transfers between devices, backward_pass(): lax.psum_scatter(partial_value.reshape(-1, width).astype(jnp.bfloat16), '...  73.8 us
    all_gather x1, waiting for transfers between devices, forward_pass(): gathered = lax.all_gather(features, 'row', axis=0, tiled=True)  52.7 us
    dot_general x8, matrix products, one_block(): jnp.einsum('bji,bjf->bif', pattern, source[block_cols], preferred_element...  23.2 us
    dot_general x8, matrix products, one_block(): jnp.einsum('bji,bif->bjf', pattern, source[block_rows], preferred_element...  21.6 us
    gather x8, local copies, waits for them, and re-layouts, one_block(): source[block_rows]  18.2 us
    gather x8, local copies, waits for them, and re-layouts, one_block(): source[block_cols]  18.2 us
  transfers between devices with their start and end apart: 5, of which 3 were waited for; matrix products, arithmetic and copies ran while one was open for 42% of the time, Pallas kernels for 0%

commit v1 on v0

--- a/solution.py
+++ b/solution.py
@@ -95,7 +95,8 @@
     local_term = lax.dot_general(
         aggregated, cotangent, (((0,), (0,)), ((), ())), preferred_element_type=jnp.float32
     )
-    weight_grad = lax.psum(local_term, ("row", "col"))
+    inner = lax.psum(local_term, "col")
+    weight_grad = lax.psum(inner, "row")
     return (output, weight_grad, input_grad)
 
 

time: 692 us -> 631 us (0.912)
  waiting for transfers between devices: 382 us -> 323 us
    psum x1 -> x2, waiting for transfers between devices: 255 us -> 94.1 us  [the longest x1 94.1 us: per_device(): weight_grad = lax.psum(inner, 'row')]
    reduce_scatter x1, waiting for transfers between devices: 0.02 us -> 57.5 us  [forward_pass(): lax.psum_scatter(partial_value.reshape(-1, width).astype(jnp.bfloat16), '...]
    all_gather x1, waiting for transfers between devices: 0.02 us -> 38.7 us  [backward_pass(): gathered = lax.all_gather(scaled, 'col', axis=0, tiled=True)]
  transfers between devices with their start and end apart: 5 -> 6, of which waited for: 3 -> 5; matrix products, arithmetic and copies ran while one was open for 42% -> 23% of each run, Pallas kernels for 0% -> 0%
where the time goes in v1:
time: 631 us; the launch traced here: 629 us
  waiting for transfers between devices  323 us (51%)
  other arithmetic  181 us (29%)
  local copies, waits for them, and re-layouts  60.8 us (10%)
  matrix products  49.6 us (8%)
  between operations  14.1 us (2%)
    scatter-add x16, other arithmetic, one_block(): return totals.at[placed].add(product)  159 us
    psum x1, waiting for transfers between devices, per_device(): weight_grad = lax.psum(inner, 'row')  94.1 us
    reduce_scatter x1, waiting for transfers between devices, backward_pass(): lax.psum_scatter(partial_value.reshape(-1, width).astype(jnp.bfloat16), '...  76.9 us
    reduce_scatter x1, waiting for transfers between devices, forward_pass(): lax.psum_scatter(partial_value.reshape(-1, width).astype(jnp.bfloat16), '...  57.5 us
    all_gather x1, waiting for transfers between devices, forward_pass(): gathered = lax.all_gather(features, 'row', axis=0, tiled=True)  55.1 us
    all_gather x1, waiting for transfers between devices, backward_pass(): gathered = lax.all_gather(scaled, 'col', axis=0, tiled=True)  38.7 us
    dot_general x8, matrix products, one_block(): jnp.einsum('bji,bjf->bif', pattern, source[block_cols], preferred_element...  23.3 us
    dot_general x8, matrix products, one_block(): jnp.einsum('bji,bif->bjf', pattern, source[block_rows], preferred_element...  21.7 us
  transfers between devices with their start and end apart: 6, of which 5 were waited for; matrix products, arithmetic and copies ran while one was open for 23% of the time, Pallas kernels for 0%

profile of v1, /device:TPU:2, one launch (start us, length us, event | category | flops | bytes accessed | tf_op | source)
XLA Modules:
  0.0 629.2 jit_solution(6512705900646291427)
XLA Ops:
  8.0 55.1 %all-gather.3.cloned.1.call-done = bf16[4096,256]{1,0:T(8,128)(2,1)} async-done(((bf16[256,256]{1,0:T(8,128)(2,1)}), bf16[4096,256]{1,0:T(8,128)(2,1)}) %all-gather.3.cloned.1.call-update) | async-done | bytes 2097168 | tf_op jit(solution)/shard_map/all_gather | solution.py:52
  63.1 2.5 broadcast.54.clone
  65.5 136.1 %while.26 = (s32[]{:T(128)}, f32[32,128,256]{2,1,0:T(8,128)}, s32[256]{0:T(256)S(1)}, s32[256,16,128]{2,1,0:T(8,128)}, s32[]{:T(128)}, /*index=5*/s32[256]{0:T(2...) while((s32[]{:T(128)}, f32[32,128,256]{2,1,0:T(8,128)}, ...), condition=%wide.region_2.3_spmd, body=%wide.region_0.2_spmd.sunk | while | flops 271582656 | bytes 23862704 | solution.py:46
  66.3 2.3 gather_fusion
  69.7 2.9 fusion.35
  72.6 10.0 %scatter_fusion = f32[32,128,256]{2,1,0:T(8,128)} fusion(f32[32,128,256]{2,1,0:T(8,128)} %get-tuple-element.398, s32[32]{0:T(128)S(1)} %get-tuple-element.375, f32[32,128,256]{2,1,0:T(8,128)} %fusion.35), kind=kCustom, calls=%fused_computation.2.clone.1 | custom fusion | flops 1048576 | bytes 12583040 | tf_op jit(solution)/shard_map/while/body/eval_jaxpr/scatter-add | solution.py:42
  83.4 2.3 gather_fusion
  86.8 2.9 fusion.35
  89.7 10.0 %scatter_fusion = f32[32,128,256]{2,1,0:T(8,128)} fusion(f32[32,128,256]{2,1,0:T(8,128)} %get-tuple-element.398, s32[32]{0:T(128)S(1)} %get-tuple-element.375, f32[32,128,256]{2,1,0:T(8,128)} %fusion.35), kind=kCustom, calls=%fused_computation.2.clone.1 | custom fusion | flops 1048576 | bytes 12583040 | tf_op jit(solution)/shard_map/while/body/eval_jaxpr/scatter-add | solution.py:42
  100.4 2.3 gather_fusion
  103.8 2.9 fusion.35
  106.7 9.8 %scatter_fusion = f32[32,128,256]{2,1,0:T(8,128)} fusion(f32[32,128,256]{2,1,0:T(8,128)} %get-tuple-element.398, s32[32]{0:T(128)S(1)} %get-tuple-element.375, f32[32,128,256]{2,1,0:T(8,128)} %fusion.35), kind=kCustom, calls=%fused_computation.2.clone.1 | custom fusion | flops 1048576 | bytes 12583040 | tf_op jit(solution)/shard_map/while/body/eval_jaxpr/scatter-add | solution.py:42
  117.3 2.3 gather_fusion
  120.6 2.9 fusion.35
  123.5 9.9 %scatter_fusion = f32[32,128,256]{2,1,0:T(8,128)} fusion(f32[32,128,256]{2,1,0:T(8,128)} %get-tuple-element.398, s32[32]{0:T(128)S(1)} %get-tuple-element.375, f32[32,128,256]{2,1,0:T(8,128)} %fusion.35), kind=kCustom, calls=%fused_computation.2.clone.1 | custom fusion | flops 1048576 | bytes 12583040 | tf_op jit(solution)/shard_map/while/body/eval_jaxpr/scatter-add | solution.py:42
  134.3 2.3 gather_fusion
  137.7 2.9 fusion.35
  140.6 9.8 %scatter_fusion = f32[32,128,256]{2,1,0:T(8,128)} fusion(f32[32,128,256]{2,1,0:T(8,128)} %get-tuple-element.398, s32[32]{0:T(128)S(1)} %get-tuple-element.375, f32[32,128,256]{2,1,0:T(8,128)} %fusion.35), kind=kCustom, calls=%fused_computation.2.clone.1 | custom fusion | flops 1048576 | bytes 12583040 | tf_op jit(solution)/shard_map/while/body/eval_jaxpr/scatter-add | solution.py:42
  151.2 2.3 gather_fusion
  154.6 2.9 fusion.35
  157.5 10.0 %scatter_fusion = f32[32,128,256]{2,1,0:T(8,128)} fusion(f32[32,128,256]{2,1,0:T(8,128)} %get-tuple-element.398, s32[32]{0:T(128)S(1)} %get-tuple-element.375, f32[32,128,256]{2,1,0:T(8,128)} %fusion.35), kind=kCustom, calls=%fused_computation.2.clone.1 | custom fusion | flops 1048576 | bytes 12583040 | tf_op jit(solution)/shard_map/while/body/eval_jaxpr/scatter-add | solution.py:42
  168.3 2.3 gather_fusion
  171.6 2.9 fusion.35
  174.5 10.1 %scatter_fusion = f32[32,128,256]{2,1,0:T(8,128)} fusion(f32[32,128,256]{2,1,0:T(8,128)} %get-tuple-element.398, s32[32]{0:T(128)S(1)} %get-tuple-element.375, f32[32,128,256]{2,1,0:T(8,128)} %fusion.35), kind=kCustom, calls=%fused_computation.2.clone.1 | custom fusion | flops 1048576 | bytes 12583040 | tf_op jit(solution)/shard_map/while/body/eval_jaxpr/scatter-add | solution.py:42
  185.4 2.3 gather_fusion
  188.8 2.9 fusion.35
  191.7 9.9 %scatter_fusion = f32[32,128,256]{2,1,0:T(8,128)} fusion(f32[32,128,256]{2,1,0:T(8,128)} %get-tuple-element.398, s32[32]{0:T(128)S(1)} %get-tuple-element.375, f32[32,128,256]{2,1,0:T(8,128)} %fusion.35), kind=kCustom, calls=%fused_computation.2.clone.1 | custom fusion | flops 1048576 | bytes 12583040 | tf_op jit(solution)/shard_map/while/body/eval_jaxpr/scatter-add | solution.py:42
  201.6 3.8 convert_element_type.63
  207.2 57.5 %reduce-scatter.3.cloned.1.call-done = bf16[256,256]{1,0:T(8,128)(2,1)} async-done(((bf16[4096,256]{1,0:T(8,128)(2,1)}), bf16[256,256]{1,0:T(8,128)(2,1)}) %reduce-scatter.3.cloned.1.call-update) | async-done | bytes 131088 | tf_op jit(solution)/shard_map/reduce_scatter | solution.py:56
  264.6 1.9 fusion.20
  266.6 38.7 %all-gather.5.cloned.1.call-done = bf16[4096,256]{1,0:T(8,128)(2,1)} async-done(((bf16[256,256]{1,0:T(8,128)(2,1)}), bf16[4096,256]{1,0:T(8,128)(2,1)}) %all-gather.5.cloned.1.call-update) | async-done | bytes 2097168 | tf_op jit(solution)/shard_map/all_gather | solution.py:73
  305.3 2.5 broadcast.54.clone.1
  307.8 134.8 %while.27 = (s32[]{:T(128)}, f32[32,128,256]{2,1,0:T(8,128)}, s32[256]{0:T(256)S(1)}, s32[256,16,128]{2,1,0:T(8,128)}, s32[]{:T(128)}, /*index=5*/s32[256]{0:T(2...) while((s32[]{:T(128)}, f32[32,128,256]{2,1,0:T(8,128)}, ...), condition=%wide.region_8.9_spmd, body=%wide.region_6.0_spmd.sunk | while | flops 271582656 | bytes 23862704 | solution.py:46
  308.6 2.3 gather_fusion.1
  311.9 2.7 fusion.38
  314.6 10.1 %scatter_fusion.1 = f32[32,128,256]{2,1,0:T(8,128)} fusion(f32[32,128,256]{2,1,0:T(8,128)} %get-tuple-element.431, s32[32]{0:T(128)S(1)} %get-tuple-element.384, f32[32,128,256]{2,1,0:T(8,128)} %fusion.38), kind=kCustom, calls=%fused_computation.3.clone.1 | custom fusion | flops 1048576 | bytes 12583040 | tf_op jit(solution)/shard_map/while/body/eval_jaxpr/scatter-add | solution.py:42
  325.6 2.3 gather_fusion.1
  327.9 1.0 constant_dynamic-slice_fusion.5
  329.0 2.7 fusion.38
  331.7 9.8 %scatter_fusion.1 = f32[32,128,256]{2,1,0:T(8,128)} fusion(f32[32,128,256]{2,1,0:T(8,128)} %get-tuple-element.431, s32[32]{0:T(128)S(1)} %get-tuple-element.384, f32[32,128,256]{2,1,0:T(8,128)} %fusion.38), kind=kCustom, calls=%fused_computation.3.clone.1 | custom fusion | flops 1048576 | bytes 12583040 | tf_op jit(solution)/shard_map/while/body/eval_jaxpr/scatter-add | solution.py:42
  342.3 2.3 gather_fusion.1
  345.6 2.7 fusion.38
  348.4 10.0 %scatter_fusion.1 = f32[32,128,256]{2,1,0:T(8,128)} fusion(f32[32,128,256]{2,1,0:T(8,128)} %get-tuple-element.431, s32[32]{0:T(128)S(1)} %get-tuple-element.384, f32[32,128,256]{2,1,0:T(8,128)} %fusion.38), kind=kCustom, calls=%fused_computation.3.clone.1 | custom fusion | flops 1048576 | bytes 12583040 | tf_op jit(solution)/shard_map/while/body/eval_jaxpr/scatter-add | solution.py:42
  359.1 2.3 gather_fusion.1
  362.5 2.7 fusion.38
  365.2 9.9 %scatter_fusion.1 = f32[32,128,256]{2,1,0:T(8,128)} fusion(f32[32,128,256]{2,1,0:T(8,128)} %get-tuple-element.431, s32[32]{0:T(128)S(1)} %get-tuple-element.384, f32[32,128,256]{2,1,0:T(8,128)} %fusion.38), kind=kCustom, calls=%fused_computation.3.clone.1 | custom fusion | flops 1048576 | bytes 12583040 | tf_op jit(solution)/shard_map/while/body/eval_jaxpr/scatter-add | solution.py:42
  375.9 2.3 gather_fusion.1
  378.2 1.0 constant_dynamic-slice_fusion.5
  379.3 2.7 fusion.38
  382.0 9.8 %scatter_fusion.1 = f32[32,128,256]{2,1,0:T(8,128)} fusion(f32[32,128,256]{2,1,0:T(8,128)} %get-tuple-element.431, s32[32]{0:T(128)S(1)} %get-tuple-element.384, f32[32,128,256]{2,1,0:T(8,128)} %fusion.38), kind=kCustom, calls=%fused_computation.3.clone.1 | custom fusion | flops 1048576 | bytes 12583040 | tf_op jit(solution)/shard_map/while/body/eval_jaxpr/scatter-add | solution.py:42
  392.6 2.3 gather_fusion.1
  396.0 2.7 fusion.38
  398.7 10.1 %scatter_fusion.1 = f32[32,128,256]{2,1,0:T(8,128)} fusion(f32[32,128,256]{2,1,0:T(8,128)} %get-tuple-element.431, s32[32]{0:T(128)S(1)} %get-tuple-element.384, f32[32,128,256]{2,1,0:T(8,128)} %fusion.38), kind=kCustom, calls=%fused_computation.3.clone.1 | custom fusion | flops 1048576 | bytes 12583040 | tf_op jit(solution)/shard_map/while/body/eval_jaxpr/scatter-add | solution.py:42
  409.6 2.3 gather_fusion.1
  412.9 2.7 fusion.38
  415.6 10.1 %scatter_fusion.1 = f32[32,128,256]{2,1,0:T(8,128)} fusion(f32[32,128,256]{2,1,0:T(8,128)} %get-tuple-element.431, s32[32]{0:T(128)S(1)} %get-tuple-element.384, f32[32,128,256]{2,1,0:T(8,128)} %fusion.38), kind=kCustom, calls=%fused_computation.3.clone.1 | custom fusion | flops 1048576 | bytes 12583040 | tf_op jit(solution)/shard_map/while/body/eval_jaxpr/scatter-add | solution.py:42
  426.5 2.3 gather_fusion.1
  429.9 2.7 fusion.38
  432.6 10.0 %scatter_fusion.1 = f32[32,128,256]{2,1,0:T(8,128)} fusion(f32[32,128,256]{2,1,0:T(8,128)} %get-tuple-element.431, s32[32]{0:T(128)S(1)} %get-tuple-element.384, f32[32,128,256]{2,1,0:T(8,128)} %fusion.38), kind=kCustom, calls=%fused_computation.3.clone.1 | custom fusion | flops 1048576 | bytes 12583040 | tf_op jit(solution)/shard_map/while/body/eval_jaxpr/scatter-add | solution.py:42
  442.6 3.8 convert_element_type.71
  447.0 76.9 %reduce-scatter.5.cloned.1.call-done = bf16[256,256]{1,0:T(8,128)(2,1)} async-done(((bf16[4096,256]{1,0:T(8,128)(2,1)}), bf16[256,256]{1,0:T(8,128)(2,1)}) %reduce-scatter.5.cloned.1.call-update) | async-done | bytes 131088 | tf_op jit(solution)/shard_map/reduce_scatter | solution.py:77
  523.9 1.8 convolution_convert_fusion
  526.6 94.1 %all-reduce.5.cloned.1.call-done = f32[256,256]{1,0:T(8,128)} async-done(((f32[256,256]{1,0:T(8,128)}), f32[256,256]{1,0:T(8,128)}) %all-reduce.5.cloned.1.call-update) | async-done | bytes 262160 | tf_op jit(solution)/shard_map/psum | solution.py:99
  620.7 1.7 copy.30
  (122 shorter events, 32.0 us)
Async XLA Ops:
  7.2 516.7 %copy-start = (bf16[256,256]{1,0:T(8,128)(2,1)S(1)}, bf16[256,256]{1,0:T(8,128)(2,1)}, u32[]{:S(2)}) copy-start(bf16[256,256]{1,0:T(8,128)(2,1)} %param.15) | copy-start | bytes 393220
  7.2 55.9 %all-gather.3.cloned.1.call-start = ((), (), s32[]{:S(2)}) async-start(), calls=%async_computation.2 | async-start | bytes 2228224 | tf_op jit(solution)/shard_map/all_gather | solution.py:52
  7.9 256.7 %reduce-scatter.3.cloned.1.call-start = ((), (), s32[]{:S(2)}) async-start(), calls=%async_computation.3 | async-start | bytes 2228224 | tf_op jit(solution)/shard_map/reduce_scatter | solution.py:56
  63.1 2.5 copy-start.2
  63.1 2.5 copy-start.3
  205.4 0.7 copy-start.4
  205.4 0.9 copy-start.1
  205.5 99.9 %all-gather.5.cloned.1.call-start = ((), (), s32[]{:S(2)}) async-start(), calls=%async_computation.6 | async-start | bytes 2228224 | tf_op jit(solution)/shard_map/all_gather | solution.py:73
  207.1 239.4 %all-reduce.3.cloned.1.call-start = ((), (), s32[]{:S(2)}) async-start(), calls=%async_computation.4 | async-start | bytes 524288 | tf_op jit(solution)/shard_map/psum | solution.py:98
  266.6 257.3 %reduce-scatter.5.cloned.1.call-start = ((), (), s32[]{:S(2)}) async-start(), calls=%async_computation.7 | async-start | bytes 2228224 | tf_op jit(solution)/shard_map/reduce_scatter | solution.py:77
  446.4 79.3 %copy-start.5 = (bf16[256,256]{1,0:T(8,128)(2,1)S(1)}, bf16[256,256]{1,0:T(8,128)(2,1)}, u32[]{:S(2)}) copy-start(bf16[256,256]{1,0:T(8,128)(2,1)} %reduce-scatter.3.cloned.1.call-done) | copy-start | bytes 393220
  446.5 174.2 %all-reduce.5.cloned.1.call-start = ((), (), s32[]{:S(2)}) async-start(), calls=%async_computation.5 | async-start | bytes 524288 | tf_op jit(solution)/shard_map/psum | solution.py:99
Sparse Core Ops, SparseCore 0:
  10.4 52.5 all-gather.2
  205.6 59.0 reduce-scatter.2
  267.1 38.2 all-gather.4
  308.1 106.7 all-reduce.2
  446.6 77.2 reduce-scatter.4
  526.9 93.6 all-reduce.4
